TPU v7x, 32 devices: a whole 2x2x4 slice. The times are simulated.
32 devices in a mesh: row: 4 (over x, core), col: 8 (over z, y).
Axes of the slice: x: 2, y: 2, z: 4, core: 2. Of those that a mesh axis runs over, the one named last changes fastest.
Arguments:
- embeddings: bfloat16 [4096, 512], P(('row', 'col')), may hold values from -6 to 6
- sketch: bfloat16 [4096, 64], P(('row', 'col')), may hold values from -240 to 240
Outputs:
- basis: float32 [4096, 64], P(('row', 'col'))
- first_pass: float32 [4096, 64], P(('row', 'col'))
All inputs are finite; a program needn't handle non-finite values.
Results may differ from a plain program's by a relative error of at most 0.00205.
Values may be sent and summed in bfloat16 or wider, within the bound.
No kernel may reach another device: no remote copies, remote signals or barrier semaphores. Data moves between devices by JAX's collectives and lax.ppermute only.
A program may use at most 64 MiB of HBM per device.

v0:
```python
import jax
import jax.numpy as jnp
from jax import lax
from jax.sharding import PartitionSpec as P


def squares_of(points):
    return jnp.sum(jnp.square(points.astype(jnp.float32)), axis=1)


def kernel_tile(left, right, left_sq, right_sq, gamma):
    cross = lax.dot_general(
        left, right, (((1,), (1,)), ((), ())), preferred_element_type=jnp.float32
    )
    dist = left_sq[:, None] + right_sq[None, :] - 2.0 * cross
    return jnp.exp(-gamma * dist).astype(jnp.bfloat16)


def product_of(left, right):
    return lax.dot_general(
        left,
        right,
        (((0,), (0,)), ((), ())),
        precision=lax.Precision.HIGHEST,
        preferred_element_type=jnp.float32,
    )


def per_device(embeddings, sketch):
    width = embeddings.shape[1]
    gamma = 3.0 / width
    own_points = lax.all_gather(embeddings, "row", axis=0, tiled=True)
    own_sq = squares_of(own_points)
    empty = jnp.zeros((own_points.shape[0], sketch.shape[1]), jnp.float32)
    total = empty
    points = lax.all_gather(embeddings, "col", axis=0, tiled=True)
    tests = lax.all_gather(sketch, "col", axis=0, tiled=True)
    count = points.shape[0]
    size = 512

    def step(carry, block):
        block_points, block_tests = block
        tile = kernel_tile(own_points, block_points, own_sq, squares_of(block_points), gamma)
        return (carry + jnp.dot(tile, block_tests, preferred_element_type=jnp.float32), None)

    stacked = (
        points.reshape(count // size, size, width),
        tests.reshape(count // size, size, tests.shape[1]),
    )
    total, unused = lax.scan(step, total, stacked)
    sketched = lax.psum_scatter(total, "row", scatter_dimension=0, tiled=True)
    core = lax.psum(product_of(sketch.astype(jnp.float32), sketched), ("row", "col"))
    lower = jnp.linalg.cholesky(core)
    first = jax.scipy.linalg.solve_triangular(lower, sketched.T, lower=True).T
    gram_two = lax.psum(product_of(first, first), ("row", "col"))
    lower_two = jnp.linalg.cholesky(gram_two)
    second = jax.scipy.linalg.solve_triangular(lower_two, first.T, lower=True).T
    total_points = sketched.shape[0] * lax.axis_size("row") * lax.axis_size("col")
    scale = jnp.sqrt(jnp.float32(total_points))
    return (second * scale, first * scale)


def solution(mesh):
    placed = (P(("row", "col"), None), P(("row", "col"), None))
    return jax.shard_map(
        per_device,
        mesh=mesh,
        in_specs=placed,
        out_specs=(P(("row", "col"), None), P(("row", "col"), None)),
        check_vma=False,
    )
```

profile of v0, /device:TPU:0, one launch (start us, length us, event | category | flops | bytes accessed | tf_op | source)
XLA Modules:
  0.0 193.4 jit_solution(8559707278417701284)
XLA Ops:
  7.2 0.7 all-gather.2.cloned.1.call-update
  8.0 28.2 %all_gather.11 = bf16[1024,64]{0,1:T(8,128)(2,1)S(1)} all-gather(bf16[128,64]{0,1:T(8,128)(2,1)S(1)} %copy-done.3), channel_id=1, replica_groups=mesh['row'=4,'col'=8] {'col'}, dimensions={0}, use_global_device_ids=true | all-gather | bytes 147456 | tf_op jit(solution)/shard_map/all_gather | solution.py:37
  36.4 0.7 copy-done
  37.1 7.2 %all_gather.9 = bf16[512,512]{1,0:T(8,128)(2,1)S(1)} all-gather(bf16[128,512]{1,0:T(8,128)(2,1)S(1)} %copy-done), channel_id=1, replica_groups=mesh['row'=4,'col'=8] {'row'}, dimensions={0}, use_global_device_ids=true | all-gather | bytes 655360 | tf_op jit(solution)/shard_map/all_gather | solution.py:32
  44.5 9.1 %all-gather.2.cloned.1.call-done = bf16[1024,512]{1,0:T(8,128)(2,1)} async-done(((bf16[128,512]{1,0:T(8,128)(2,1)}), bf16[1024,512]{1,0:T(8,128)(2,1)}) %all-gather.2.cloned.1.call-update) | async-done | bytes 1048592 | tf_op jit(solution)/shard_map/all_gather | solution.py:36
  53.6 6.2 %while.11 = (s32[]{:T(128)}, f32[512,64]{0,1:T(8,128)S(1)}, f32[512]{0:T(512)S(1)}, bf16[2,512,512]{2,1,0:T(8,128)(2,1)}, bf16[512,512]{1,0:T(8,128)(2,1)S(1)}, ...) while((s32[]{:T(128)}, f32[512,64]{0,1:T(8,128)S(1)}, f32[512]{0:T(512)S(1)}, ...), condition=%wide.region_3.4_spmd.clone, body=%wide.region_1.3_spmd.clone.sunk | while | flops 304152064 | bytes 1973347 | solution.py:50
  53.6 1.2 multiply_reduce_fusion.3
  54.8 1.8 fusion.47
  56.6 1.2 multiply_reduce_fusion.3
  57.9 1.8 fusion.47
  59.7 0.6 copy-done.2
  60.4 18.5 %reduce-scatter.2.cloned.1.call-done = f32[128,64]{0,1:T(8,128)} async-done(((f32[512,64]{0,1:T(8,128)}), f32[128,64]{0,1:T(8,128)}) %reduce-scatter.2.cloned.1.call-update) | async-done | bytes 32784 | tf_op jit(solution)/shard_map/reduce_scatter | solution.py:51
  78.9 0.9 convolution_bitcast_fusion
  79.8 39.4 %psum.14 = f32[64,64]{0,1:T(8,128)S(1)} all-reduce(f32[64,64]{0,1:T(8,128)S(1)} %convolution_bitcast_fusion), channel_id=1, replica_groups=mesh['row'=4,'col'=8] {'row','col'}, use_global_device_ids=true, to_apply=%region_5.6 | all-reduce | flops 4096 | bytes 32768 | tf_op jit(solution)/shard_map/psum | solution.py:52
  119.3 5.8 %cholesky.44 = f32[64,64]{1,0:T(8,128)S(1)} custom-call(f32[64,64]{1,0:T(8,128)S(1)} %fusion.30), custom_call_target="Cholesky" | custom-call | tf_op jit(solution)/shard_map/jit(cholesky)/cholesky | solution.py:53
  125.2 0.6 compare_reduce_fusion.1
  125.9 0.7 fusion.23
  126.5 4.9 %custom-call.7 = f32[1,64,64]{1,2,0:T(8,128)S(1)} custom-call(f32[1,64,64]{2,1,0:T(8,128)S(1)} %fusion.23), custom_call_target="InvertDiagBlocksLowerTriangular" | custom-call | tf_op jit(solution)/shard_map/jit(_solve_triangular)/triangular_solve | solution.py:54
  132.5 41.0 %psum.15 = f32[64,64]{0,1:T(8,128)S(1)} all-reduce(f32[64,64]{0,1:T(8,128)S(1)} %fusion.33), channel_id=1, replica_groups=mesh['row'=4,'col'=8] {'row','col'}, use_global_device_ids=true, to_apply=%region_8.11 | all-reduce | flops 4096 | bytes 32768 | tf_op jit(solution)/shard_map/psum | solution.py:55
  173.6 5.8 %cholesky.55 = f32[64,64]{1,0:T(8,128)S(1)} custom-call(f32[64,64]{1,0:T(8,128)S(1)} %fusion.26), custom_call_target="Cholesky" | custom-call | tf_op jit(solution)/shard_map/jit(cholesky)/cholesky | solution.py:56
  179.5 0.6 compare_reduce_fusion
  180.2 0.7 fusion.24
  180.8 4.9 %custom-call.8 = f32[1,64,64]{1,2,0:T(8,128)S(1)} custom-call(f32[1,64,64]{2,1,0:T(8,128)S(1)} %fusion.24), custom_call_target="InvertDiagBlocksLowerTriangular" | custom-call | tf_op jit(solution)/shard_map/jit(_solve_triangular)/triangular_solve | solution.py:57
  185.7 0.9 fusion.22
  (21 shorter events, 1.7 us)
Async XLA Ops:
  7.2 0.8 copy-start.3
  7.2 46.4 %all-gather.2.cloned.1.call-start = ((), (), s32[]{:S(2)}) async-start(), calls=%async_computation.1 | async-start | bytes 1179648 | tf_op jit(solution)/shard_map/all_gather | solution.py:36
  7.9 71.0 %reduce-scatter.2.cloned.1.call-start = ((), (), s32[]{:S(2)}) async-start(), calls=%async_computation.2 | async-start | bytes 163840 | tf_op jit(solution)/shard_map/reduce_scatter | solution.py:51
  36.2 0.9 copy-start
  59.7 0.6 copy-start.2
  125.9 5.6 %copy-start.1 = (f32[128,64]{0,1:T(8,128)S(1)}, f32[128,64]{0,1:T(8,128)}, u32[]{:S(2)}) copy-start(f32[128,64]{0,1:T(8,128)} %reduce-scatter.2.cloned.1.call-done) | copy-start | bytes 98308
Sparse Core Ops, SparseCore 0:
  10.1 43.4 all-gather.1
  60.5 18.3 reduce-scatter.1
where the time goes:
time: 194 us; the launch traced here: 193 us
  blocking collectives  116 us (60%)
  waiting for transfers between devices  28.3 us (15%)
  other arithmetic  27.4 us (14%)
  between operations  14.2 us (7%)
  matrix products  5.88 us (3%)
    psum x1, blocking collectives, per_device(): gram_two = lax.psum(product_of(first, first), ('row', 'col'))  41 us
    psum x1, blocking collectives, per_device(): lax.psum(product_of(sketch.astype(jnp.float32), sketched), ('row', 'col'))  39.4 us
    all_gather x1, blocking collectives, per_device(): tests = lax.all_gather(sketch, 'col', axis=0, tiled=True)  28.2 us
    reduce_scatter x1, waiting for transfers between devices, per_device(): sketched = lax.psum_scatter(total, 'row', scatter_dimension=0, tiled=True)  18.5 us
    all_gather x1, waiting for transfers between devices, per_device(): points = lax.all_gather(embeddings, 'col', axis=0, tiled=True)  9.11 us
    all_gather x1, blocking collectives, per_device(): own_points = lax.all_gather(embeddings, 'row', axis=0, tiled=True)  7.18 us
    another operation x3, other arithmetic, per_device(): lower_two = jnp.linalg.cholesky(gram_two)  6.52 us
    another operation x3, other arithmetic, per_device(): lower = jnp.linalg.cholesky(core)  6.52 us
  transfers between devices with their start and end apart: 2, of which 2 were waited for; matrix products, arithmetic and copies ran while one was open for 0% of the time, Pallas kernels for 0%

commit v1 on v0

--- a/solution.py
+++ b/solution.py
@@ -52,7 +52,7 @@
     core = lax.psum(product_of(sketch.astype(jnp.float32), sketched), ("row", "col"))
     lower = jnp.linalg.cholesky(core)
     first = jax.scipy.linalg.solve_triangular(lower, sketched.T, lower=True).T
-    gram_two = lax.psum(product_of(first, first), ("row", "col"))
+    gram_two = lax.psum(lax.psum(product_of(first, first), "col"), "row")
     lower_two = jnp.linalg.cholesky(gram_two)
     second = jax.scipy.linalg.solve_triangular(lower_two, first.T, lower=True).T
     total_points = sketched.shape[0] * lax.axis_size("row") * lax.axis_size("col")

time: 194 us -> 200 us (1.031)
  blocking collectives: 116 us -> 122 us
    psum x1 -> x2, blocking collectives: 41 us -> 47.1 us  [per_device(): gram_two = lax.psum(lax.psum(product_of(first, first), 'col'), 'row')]
where the time goes in v1:
time: 200 us; the launch traced here: 199 us
  blocking collectives  122 us (61%)
  waiting for transfers between devices  28.3 us (14%)
  other arithmetic  27.4 us (14%)
  between operations  14.2 us (7%)
  matrix products  5.88 us (3%)
    psum x2, blocking collectives, per_device(): gram_two = lax.psum(lax.psum(product_of(first, first), 'col'), 'row')  47.1 us
    psum x1, blocking collectives, per_device(): lax.psum(product_of(sketch.astype(jnp.float32), sketched), ('row', 'col'))  39.4 us
    all_gather x1, blocking collectives, per_device(): tests = lax.all_gather(sketch, 'col', axis=0, tiled=True)  28.2 us
    reduce_scatter x1, waiting for transfers between devices, per_device(): sketched = lax.psum_scatter(total, 'row', scatter_dimension=0, tiled=True)  18.5 us
    all_gather x1, waiting for transfers between devices, per_device(): points = lax.all_gather(embeddings, 'col', axis=0, tiled=True)  9.11 us
    all_gather x1, blocking collectives, per_device(): own_points = lax.all_gather(embeddings, 'row', axis=0, tiled=True)  7.18 us
    another operation x3, other arithmetic, per_device(): lower = jnp.linalg.cholesky(core)  6.52 us
    another operation x3, other arithmetic, per_device(): lower_two = jnp.linalg.cholesky(gram_two)  6.52 us
  transfers between devices with their start and end apart: 2, of which 2 were waited for; matrix products, arithmetic and copies ran while one was open for 0% of the time, Pallas kernels for 0%

profile of v1, /device:TPU:0, one launch (start us, length us, event | category | flops | bytes accessed | tf_op | source)
XLA Modules:
  0.0 199.5 jit_solution(7991163948288984322)
XLA Ops:
  7.2 0.7 all-gather.2.cloned.1.call-update
  8.0 28.2 %all_gather.11 = bf16[1024,64]{0,1:T(8,128)(2,1)S(1)} all-gather(bf16[128,64]{0,1:T(8,128)(2,1)S(1)} %copy-done.3), channel_id=1, replica_groups=mesh['row'=4,'col'=8] {'col'}, dimensions={0}, use_global_device_ids=true | all-gather | bytes 147456 | tf_op jit(solution)/shard_map/all_gather | solution.py:37
  36.4 0.7 copy-done
  37.1 7.2 %all_gather.9 = bf16[512,512]{1,0:T(8,128)(2,1)S(1)} all-gather(bf16[128,512]{1,0:T(8,128)(2,1)S(1)} %copy-done), channel_id=1, replica_groups=mesh['row'=4,'col'=8] {'row'}, dimensions={0}, use_global_device_ids=true | all-gather | bytes 655360 | tf_op jit(solution)/shard_map/all_gather | solution.py:32
  44.5 9.1 %all-gather.2.cloned.1.call-done = bf16[1024,512]{1,0:T(8,128)(2,1)} async-done(((bf16[128,512]{1,0:T(8,128)(2,1)}), bf16[1024,512]{1,0:T(8,128)(2,1)}) %all-gather.2.cloned.1.call-update) | async-done | bytes 1048592 | tf_op jit(solution)/shard_map/all_gather | solution.py:36
  53.6 6.2 %while.11 = (s32[]{:T(128)}, f32[512,64]{0,1:T(8,128)S(1)}, f32[512]{0:T(512)S(1)}, bf16[2,512,512]{2,1,0:T(8,128)(2,1)}, bf16[512,512]{1,0:T(8,128)(2,1)S(1)}, ...) while((s32[]{:T(128)}, f32[512,64]{0,1:T(8,128)S(1)}, f32[512]{0:T(512)S(1)}, ...), condition=%wide.region_3.4_spmd.clone, body=%wide.region_1.3_spmd.clone.sunk | while | flops 304152064 | bytes 1973347 | solution.py:50
  53.6 1.2 multiply_reduce_fusion.3
  54.8 1.8 fusion.47
  56.6 1.2 multiply_reduce_fusion.3
  57.9 1.8 fusion.47
  60.4 18.5 %reduce-scatter.2.cloned.1.call-done = f32[128,64]{0,1:T(8,128)} async-done(((f32[512,64]{0,1:T(8,128)}), f32[128,64]{0,1:T(8,128)}) %reduce-scatter.2.cloned.1.call-update) | async-done | bytes 32784 | tf_op jit(solution)/shard_map/reduce_scatter | solution.py:51
  78.9 0.9 convolution_bitcast_fusion
  79.8 39.4 %psum.21 = f32[64,64]{0,1:T(8,128)S(1)} all-reduce(f32[64,64]{0,1:T(8,128)S(1)} %convolution_bitcast_fusion), channel_id=1, replica_groups=mesh['row'=4,'col'=8] {'row','col'}, use_global_device_ids=true, to_apply=%region_5.6 | all-reduce | flops 4096 | bytes 32768 | tf_op jit(solution)/shard_map/psum | solution.py:52
  119.3 5.8 %cholesky.44 = f32[64,64]{1,0:T(8,128)S(1)} custom-call(f32[64,64]{1,0:T(8,128)S(1)} %fusion.30), custom_call_target="Cholesky" | custom-call | tf_op jit(solution)/shard_map/jit(cholesky)/cholesky | solution.py:53
  125.2 0.6 compare_reduce_fusion.1
  125.9 0.7 fusion.23
  126.5 4.9 %custom-call.7 = f32[1,64,64]{1,2,0:T(8,128)S(1)} custom-call(f32[1,64,64]{2,1,0:T(8,128)S(1)} %fusion.23), custom_call_target="InvertDiagBlocksLowerTriangular" | custom-call | tf_op jit(solution)/shard_map/jit(_solve_triangular)/triangular_solve | solution.py:54
  132.5 36.8 %psum.22 = f32[64,64]{0,1:T(8,128)S(1)} all-reduce(f32[64,64]{0,1:T(8,128)S(1)} %fusion.33), channel_id=1, replica_groups=mesh['row'=4,'col'=8] {'col'}, use_global_device_ids=true, to_apply=%region_8.11 | all-reduce | flops 4096 | bytes 32768 | tf_op jit(solution)/shard_map/psum | solution.py:55
  169.3 10.3 %psum.23 = f32[64,64]{0,1:T(8,128)S(1)} all-reduce(f32[64,64]{0,1:T(8,128)S(1)} %psum.22), channel_id=1, replica_groups=mesh['row'=4,'col'=8] {'row'}, use_global_device_ids=true, to_apply=%region_9.12 | all-reduce | flops 4096 | bytes 32768 | tf_op jit(solution)/shard_map/psum | solution.py:55
  179.7 5.8 %cholesky.55 = f32[64,64]{1,0:T(8,128)S(1)} custom-call(f32[64,64]{1,0:T(8,128)S(1)} %fusion.26), custom_call_target="Cholesky" | custom-call | tf_op jit(solution)/shard_map/jit(cholesky)/cholesky | solution.py:56
  185.6 0.6 compare_reduce_fusion
  186.2 0.7 fusion.24
  186.9 4.9 %custom-call.8 = f32[1,64,64]{1,2,0:T(8,128)S(1)} custom-call(f32[1,64,64]{2,1,0:T(8,128)S(1)} %fusion.24), custom_call_target="InvertDiagBlocksLowerTriangular" | custom-call | tf_op jit(solution)/shard_map/jit(_solve_triangular)/triangular_solve | solution.py:57
  191.8 0.9 fusion.22
  (22 shorter events, 2.4 us)
Async XLA Ops:
  7.2 0.8 copy-start.3
  7.2 46.4 %all-gather.2.cloned.1.call-start = ((), (), s32[]{:S(2)}) async-start(), calls=%async_computation.1 | async-start | bytes 1179648 | tf_op jit(solution)/shard_map/all_gather | solution.py:36
  7.9 71.0 %reduce-scatter.2.cloned.1.call-start = ((), (), s32[]{:S(2)}) async-start(), calls=%async_computation.2 | async-start | bytes 163840 | tf_op jit(solution)/shard_map/reduce_scatter | solution.py:51
  36.2 0.9 copy-start
  59.7 0.6 copy-start.2
  125.9 5.6 %copy-start.1 = (f32[128,64]{0,1:T(8,128)S(1)}, f32[128,64]{0,1:T(8,128)}, u32[]{:S(2)}) copy-start(f32[128,64]{0,1:T(8,128)} %reduce-scatter.2.cloned.1.call-done) | copy-start | bytes 98308
Sparse Core Ops, SparseCore 0:
  10.1 43.4 all-gather.1
  60.5 18.3 reduce-scatter.1
